TPU v7x, 32 devices: a whole 2x2x4 slice. The times are simulated.
32 devices in a mesh: ulysses: 4 (over z), blk: 2 (over y), tensor: 4 (over x, core).
Axes of the slice: x: 2, y: 2, z: 4, core: 2. Of those that a mesh axis runs over, the one named last changes fastest.
Arguments:
- tokens: bfloat16 [2048, 5120], P(('ulysses', 'blk'), 'tensor'), may hold values from -20 to 20
- w_qkv: bfloat16 [5120, 3, 4096], P(None, None, ('ulysses', 'tensor')), may hold values from -2 to 2
- qkv_scale: float32 [3, 32], P(None, ('ulysses', 'tensor')), may hold values from 0.6 to 9
- block_mask: int32 [32, 16, 16], P(('ulysses', 'tensor')), may hold values from 0 to 1, as said below
- w_out: bfloat16 [4, 1024, 5120], P(None, 'tensor'), may hold values from -0.125 to 0.125
Outputs:
- mixed: bfloat16 [2048, 5120], P(('ulysses', 'blk'), 'tensor')
Inputs may be any that keep to these rules, and one draw needn't show every extreme that they name: `block_mask`: 0 or 1; the share of ones differs from head to head.
All inputs are finite; a program needn't handle non-finite values.
Results may differ from a plain program's by a relative error of at most 0.015.
Values may be sent and summed in bfloat16 or wider, within the bound.
A program may use at most 128 MiB of HBM per device.

v0:
```python
import math
import jax
import jax.numpy as jnp
from jax import lax
from jax.sharding import PartitionSpec as P


def local(tokens, w_qkv, qkv_scale, block_mask, w_out):
    group_count = lax.axis_size("ulysses")
    tensor_count = lax.axis_size("tensor")
    cycle_count = lax.axis_size("blk")
    tok_rows, feat_cols = tokens.shape
    width_all, triple, head_cols = w_qkv.shape
    heads_here = qkv_scale.shape[1]
    head_dim = head_cols // heads_here
    blocks_all = block_mask.shape[1]
    group_rows = tok_rows * group_count
    block_rows = cycle_count * group_rows // blocks_all
    start_sum = jnp.zeros((group_count, tok_rows, triple, head_cols), jnp.float32)
    pieces = lax.all_gather(tokens[None], ("ulysses", "tensor"), axis=0, tiled=True)

    def one_shard(which, accum):
        group_id = which // tensor_count
        feature_id = which % tensor_count
        weights = lax.dynamic_slice_in_dim(w_qkv, feature_id * feat_cols, feat_cols, 0)
        token_part = lax.dynamic_index_in_dim(pieces, which, 0, keepdims=False)
        product = jnp.einsum("rd,dcn->rcn", token_part, weights, preferred_element_type=jnp.float32)
        current = lax.dynamic_index_in_dim(accum, group_id, 0, keepdims=False)
        return lax.dynamic_update_index_in_dim(accum, current + product, group_id, 0)

    projected = lax.fori_loop(0, pieces.shape[0], one_shard, start_sum)
    projected = (
        projected.reshape(group_rows, triple, heads_here, head_dim) * qkv_scale[None, :, :, None]
    )
    projected = projected.astype(jnp.bfloat16)
    queries = projected[:, 0]
    keys = projected[:, 1]
    values = projected[:, 2]
    cycle_index = lax.axis_index("blk")
    local_rows = jnp.arange(group_rows, dtype=jnp.int32)
    query_pos = (
        local_rows // tok_rows * cycle_count + cycle_index
    ) * tok_rows + local_rows % tok_rows
    query_block = query_pos // block_rows
    block_ids = jnp.arange(blocks_all, dtype=jnp.int32)
    query_onehot = (query_block[:, None] == block_ids[None, :]).astype(jnp.bfloat16)
    query_live = jnp.einsum(
        "qn,hnm->hqm",
        query_onehot,
        block_mask.astype(jnp.bfloat16),
        preferred_element_type=jnp.float32,
    ).astype(jnp.bfloat16)
    score_scale = 1.0 / math.sqrt(head_dim)
    start_state = (
        jnp.full((heads_here, group_rows), -1e30, jnp.float32),
        jnp.zeros((heads_here, group_rows), jnp.float32),
        jnp.zeros((heads_here, group_rows, head_dim), jnp.float32),
    )
    key_all = lax.all_gather(keys, "blk", axis=0, tiled=True)
    value_all = lax.all_gather(values, "blk", axis=0, tiled=True)

    def one_block(which, state):
        highest, denominator, numerator = state
        key_part = lax.dynamic_slice_in_dim(key_all, which * group_rows, group_rows, 0)
        value_part = lax.dynamic_slice_in_dim(value_all, which * group_rows, group_rows, 0)
        gathered_row = which * group_rows + local_rows
        owner_cycle = gathered_row // group_rows
        inner_row = gathered_row % group_rows
        key_pos = (
            inner_row // tok_rows * cycle_count + owner_cycle
        ) * tok_rows + inner_row % tok_rows
        key_block = key_pos // block_rows
        key_onehot = (key_block[:, None] == block_ids[None, :]).astype(jnp.bfloat16)
        allowed = (
            jnp.einsum("hqn,kn->hqk", query_live, key_onehot, preferred_element_type=jnp.float32)
            > 0.5
        )
        allowed = allowed | (query_block[:, None] == key_block[None, :])[None]
        scores = (
            jnp.einsum("qhd,khd->hqk", queries, key_part, preferred_element_type=jnp.float32)
            * score_scale
        )
        scores = jnp.where(allowed, scores, -jnp.inf)
        new_high = jnp.maximum(highest, jnp.max(scores, axis=-1))
        weights = jnp.exp(scores - new_high[..., None])
        factor = jnp.exp(highest - new_high)
        denominator = denominator * factor + jnp.sum(weights, axis=-1)
        numerator = numerator * factor[..., None] + jnp.einsum(
            "hqk,khd->hqd",
            weights.astype(jnp.bfloat16),
            value_part,
            preferred_element_type=jnp.float32,
        )
        return (new_high, denominator, numerator)

    highest, denominator, numerator = lax.fori_loop(
        0, key_all.shape[0] // group_rows, one_block, start_state
    )
    attended = (numerator / denominator[..., None]).astype(jnp.bfloat16)
    grouped = attended.reshape(heads_here, group_count, tok_rows, head_dim)
    arrived = lax.all_to_all(grouped, "ulysses", split_axis=1, concat_axis=0, tiled=True)
    out_rows = w_out.reshape(group_count * heads_here, head_dim, w_out.shape[2])
    partial_value = jnp.einsum(
        "grd,gdf->rf", arrived[:, 0], out_rows, preferred_element_type=jnp.float32
    )
    summed = lax.psum_scatter(
        partial_value.astype(jnp.bfloat16), "tensor", scatter_dimension=1, tiled=True
    )
    return summed


def solution(mesh):
    return jax.shard_map(
        local,
        mesh=mesh,
        in_specs=(
            P(("ulysses", "blk"), "tensor"),
            P(None, None, ("ulysses", "tensor")),
            P(None, ("ulysses", "tensor")),
            P(("ulysses", "tensor"), None, None),
            P(None, "tensor", None),
        ),
        out_specs=P(("ulysses", "blk"), "tensor"),
        check_vma=False,
    )
```

profile of v0, /device:TPU:0, one launch (start us, length us, event | category | flops | bytes accessed | tf_op | source)
XLA Modules:
  0.0 308.4 jit_solution(13720380740776168870)
XLA Ops:
  6.5 0.7 all-gather.7.cloned.1.call-update
  7.3 0.8 copy.21
  8.1 91.8 %all-gather.7.cloned.1.call-done = bf16[4096,1280]{1,0:T(8,128)(2,1)} async-done(((bf16[256,1280]{1,0:T(8,128)(2,1)}), bf16[4096,1280]{1,0:T(8,128)(2,1)}) %all-gather.7.cloned.1.call-update) | async-done | bytes 10485776 | tf_op jit(solution)/shard_map/all_gather | solution.py:20
  99.9 0.3 broadcast_in_dim.66.clone
  100.1 57.4 %while.36 = (s32[]{:T(128)}, f32[4,256,3,256]{3,1,0,2:T(8,128)S(1)}, bf16[16,256,1280]{2,1,0:T(8,128)(2,1)}, bf16[5120,3,256]{2,0,1:T(8,128)(2,1)}, s32[]{:T(128...) while((s32[]{:T(128)}, ...), condition=%wide.region_1.2_spmd, body=%wide.region_0.1_spmd.sunk | while | flops 503513120 | bytes 5768004 | solution.py:31
  100.2 0.9 constant_dynamic-slice_fusion.5
  101.1 2.6 fusion.106
  103.8 0.9 constant_dynamic-slice_fusion.5
  104.7 2.6 fusion.106
  107.3 0.9 constant_dynamic-slice_fusion.5
  108.3 2.6 fusion.106
  110.9 0.9 constant_dynamic-slice_fusion.5
  111.9 2.6 fusion.106
  114.5 0.9 constant_dynamic-slice_fusion.5
  115.5 2.6 fusion.106
  118.1 0.9 constant_dynamic-slice_fusion.5
  119.1 2.6 fusion.106
  121.7 0.9 constant_dynamic-slice_fusion.5
  122.6 2.6 fusion.106
  125.3 0.9 constant_dynamic-slice_fusion.5
  126.2 2.6 fusion.106
  128.9 0.9 constant_dynamic-slice_fusion.5
  129.8 2.6 fusion.106
  132.5 0.9 constant_dynamic-slice_fusion.5
  133.4 2.6 fusion.106
  136.0 0.9 constant_dynamic-slice_fusion.5
  137.0 2.6 fusion.106
  139.6 0.9 constant_dynamic-slice_fusion.5
  140.6 2.6 fusion.106
  143.2 0.9 constant_dynamic-slice_fusion.5
  144.2 2.6 fusion.106
  146.8 0.9 constant_dynamic-slice_fusion.5
  147.8 2.6 fusion.106
  150.4 0.9 constant_dynamic-slice_fusion.5
  151.3 2.6 fusion.106
  154.0 0.9 constant_dynamic-slice_fusion.5
  154.9 2.6 fusion.106
  157.6 3.0 reshape.217
  160.6 3.0 multiply_convert_fusion
  163.6 2.1 slice_bitcast_fusion
  165.8 0.7 all-gather.11.cloned.1.call-update
  166.6 0.1 copy.19
  166.7 0.2 fusion.69
  166.9 18.5 %all-gather.9.cloned.1.call-done = bf16[2048,1,2,128]{3,2,1,0:T(2,128)(2,1)} async-done(((bf16[1024,1,2,128]{3,2,1,0:T(2,128)(2,1)}), bf16[2048,1,2,128]{3,2,1,0:T(2,128)(2,1)}) %all-gather.9.cloned.1.call-update) | async-done | bytes 1048592 | tf_op jit(solution)/shard_map/all_gather | solution.py:59
  185.4 22.9 %all-gather.11.cloned.1.call-done = bf16[2048,1,2,128]{3,2,1,0:T(2,128)(2,1)} async-done(((bf16[1024,1,2,128]{3,2,1,0:T(2,128)(2,1)}), bf16[2048,1,2,128]{3,2,1,0:T(2,128)(2,1)}) %all-gather.11.cloned.1.call-update) | async-done | bytes 1048592 | tf_op jit(solution)/shard_map/all_gather | solution.py:60
  208.3 33.7 %while.37 = (s32[]{:T(128)}, f32[2,1024]{1,0:T(2,128)S(1)}, f32[2,1024]{1,0:T(2,128)S(1)}, f32[2,1024,128]{2,1,0:T(8,128)S(1)}, bf16[2,1024,16]{1,2,0:T(8,128)(2...) while((s32[]{:T(128)}, f32[2,1024]{1,0:T(2,128)S(1)}, ...), condition=%wide.region_5.6_spmd.clone, body=%wide.region_2.5_spmd.clone.sunk | while | flops 1161677824 | bytes 83579104 | solution.py:96
  208.3 1.9 constant_dynamic-slice_fusion.6
  210.2 0.7 broadcast_compare_fusion.2
  210.9 1.3 fusion.112
  212.2 4.8 %fusion.113 = (f32[2,1024]{1,0:T(2,128)S(1)}, f32[2,1024,1024]{1,2,0:T(8,128)}) fusion(bf16[1024,2,128]{2,0,1:T(8,128)(2,1)S(1)} %get-tuple-element.690, bf16[1024,2,128]{2,1,0:T(2,128)(2,1)S(1)} %get-tuple-element.614, pred[1024,1024]{0,1:T(8,128)(4,1)S(1)} %broadcast_compare_fusion.2, f32[1024,2,1024]{2,0,1:T(8,128)S(1)} %fusion.112), kind=kOutput, calls=%fused_computation.126.clone.1 | convolution fusion | flops 547354624 | bytes 18882560 | tf_op jit(solution)/shard_map/while/body/eval_jaxpr/qhd,khd->hqk/dot_general | solution.py:80
  217.0 4.7 %fusion.115 = f32[2,1024]{1,0:T(2,128)S(1)} fusion(f32[2,1024,1024]{1,2,0:T(8,128)} %get-tuple-element.618, f32[2,1024]{1,0:T(2,128)S(1)} %fusion.114), kind=kLoop, calls=%fused_computation.16.clone.1 | loop fusion | flops 4192256 | bytes 8404992 | tf_op jit(solution)/shard_map/while/body/eval_jaxpr/reduce_sum | solution.py:87
  221.7 1.0 copy-done
  222.7 2.3 fusion.117
  225.1 1.9 constant_dynamic-slice_fusion.6
  227.1 0.7 broadcast_compare_fusion.2
  227.7 1.3 fusion.112
  229.0 4.8 %fusion.113 = (f32[2,1024]{1,0:T(2,128)S(1)}, f32[2,1024,1024]{1,2,0:T(8,128)}) fusion(bf16[1024,2,128]{2,0,1:T(8,128)(2,1)S(1)} %get-tuple-element.690, bf16[1024,2,128]{2,1,0:T(2,128)(2,1)S(1)} %get-tuple-element.614, pred[1024,1024]{0,1:T(8,128)(4,1)S(1)} %broadcast_compare_fusion.2, f32[1024,2,1024]{2,0,1:T(8,128)S(1)} %fusion.112), kind=kOutput, calls=%fused_computation.126.clone.1 | convolution fusion | flops 547354624 | bytes 18882560 | tf_op jit(solution)/shard_map/while/body/eval_jaxpr/qhd,khd->hqk/dot_general | solution.py:80
  233.8 4.7 %fusion.115 = f32[2,1024]{1,0:T(2,128)S(1)} fusion(f32[2,1024,1024]{1,2,0:T(8,128)} %get-tuple-element.618, f32[2,1024]{1,0:T(2,128)S(1)} %fusion.114), kind=kLoop, calls=%fused_computation.16.clone.1 | loop fusion | flops 4192256 | bytes 8404992 | tf_op jit(solution)/shard_map/while/body/eval_jaxpr/reduce_sum | solution.py:87
  238.6 1.0 copy-done
  239.6 2.3 fusion.117
  242.0 0.3 divide_convert_fusion
  242.3 18.7 %all_to_all.15 = bf16[2,4,256,128]{3,2,0,1:T(8,128)(2,1)S(1)} all-to-all(bf16[2,4,256,128]{3,2,0,1:T(8,128)(2,1)S(1)} %copy.27), channel_id=1, replica_groups=mesh['ulysses'=4,'blk'=2,'tensor'=4] {'ulysses'}, dimensions={1} | all-to-all | bytes 1048576 | tf_op jit(solution)/shard_map/all_to_all | solution.py:101
  261.1 8.1 %fusion.68 = bf16[256,5120]{1,0:T(8,128)(2,1)} fusion(bf16[8,256,128]{2,1,0:T(8,128)(2,1)S(1)} %bitcast.73, bf16[8,128,5120]{2,1,0:T(8,128)(2,1)} %bitcast.76), kind=kOutput, calls=%fused_computation.94 | convolution fusion | flops 2685665280 | bytes 13631488 | tf_op jit(solution)/shard_map/grd,gdf->rf/dot_general | solution.py:103
  269.2 32.7 %reduce-scatter.2.cloned.1.call-done = bf16[256,1280]{1,0:T(8,128)(2,1)} async-done(((bf16[256,5120]{1,0:T(8,128)(2,1)}), bf16[256,1280]{1,0:T(8,128)(2,1)}) %reduce-scatter.2.cloned.1.call-update) | async-done | bytes 655376 | tf_op jit(solution)/shard_map/reduce_scatter | solution.py:106
  (26 shorter events, 0.4 us)
Async XLA Ops:
  6.5 93.3 %all-gather.7.cloned.1.call-start = ((), (), s32[]{:S(2)}) async-start(), calls=%async_computation.3 | async-start | bytes 11141120 | tf_op jit(solution)/shard_map/all_gather | solution.py:20
  7.3 178.2 %all-gather.9.cloned.1.call-start = ((), (), s32[]{:S(2)}) async-start(), calls=%async_computation.4 | async-start | bytes 1572864 | tf_op jit(solution)/shard_map/all_gather | solution.py:59
  157.5 9.0 %copy-start.1 = (s32[2,16,16]{2,1,0:T(8,128)S(1)}, s32[2,16,16]{2,1,0:T(8,128)}, u32[]{:S(2)}) copy-start(s32[2,16,16]{2,1,0:T(8,128)} %param.12) | copy-start | bytes 6148
  165.7 42.6 %all-gather.11.cloned.1.call-start = ((), (), s32[]{:S(2)}) async-start(), calls=%async_computation.5 | async-start | bytes 1572864 | tf_op jit(solution)/shard_map/all_gather | solution.py:60
  166.5 135.4 %reduce-scatter.2.cloned.1.call-start = ((), (), s32[]{:S(2)}) async-start(), calls=%async_computation.2 | async-start | bytes 3276800 | tf_op jit(solution)/shard_map/reduce_scatter | solution.py:106
  217.0 5.8 %copy-start = (f32[2,1024,1024]{1,2,0:T(8,128)S(1)}, f32[2,1024,1024]{1,2,0:T(8,128)}, u32[]{:S(2)}) copy-start(f32[2,1024,1024]{1,2,0:T(8,128)} %get-tuple-element.618) | copy-start | bytes 25165828 | tf_op jit(solution)/shard_map/while
  233.8 5.8 %copy-start = (f32[2,1024,1024]{1,2,0:T(8,128)S(1)}, f32[2,1024,1024]{1,2,0:T(8,128)}, u32[]{:S(2)}) copy-start(f32[2,1024,1024]{1,2,0:T(8,128)} %get-tuple-element.618) | copy-start | bytes 25165828 | tf_op jit(solution)/shard_map/while
Sparse Core Ops, SparseCore 0:
  9.6 90.2 all-gather.6
  165.8 19.5 all-gather.8
  187.0 21.2 all-gather.10
  269.4 32.4 reduce-scatter.1
where the time goes:
time: 309 us; the launch traced here: 308 us
  waiting for transfers between devices  167 us (54%)
  matrix products  66.7 us (22%)
  local copies, waits for them, and re-layouts  27.4 us (9%)
  blocking collectives  18.7 us (6%)
  other arithmetic  14.2 us (5%)
  between operations  13.2 us (4%)
    all_gather x1, waiting for transfers between devices, local(): lax.all_gather(tokens[None], ('ulysses', 'tensor'), axis=0, tiled=True)  91.8 us
    dot_general x16, matrix products, one_shard(): jnp.einsum('rd,dcn->rcn', token_part, weights, preferred_element_type=jnp...  41.7 us
    reduce_scatter x1, waiting for transfers between devices, local(): lax.psum_scatter(partial_value.astype(jnp.bfloat16), 'tensor', scatter_di...  32.7 us
    all_gather x1, waiting for transfers between devices, local(): value_all = lax.all_gather(values, 'blk', axis=0, tiled=True)  22.9 us
    all_to_all x1, blocking collectives, local(): lax.all_to_all(grouped, 'ulysses', split_axis=1, concat_axis=0, tiled=True)  18.7 us
    all_gather x1, waiting for transfers between devices, local(): key_all = lax.all_gather(keys, 'blk', axis=0, tiled=True)  18.5 us
    dynamic_slice x16, local copies, waits for them, and re-layouts, one_shard(): current = lax.dynamic_index_in_dim(accum, group_id, 0, keepdims=False)  15.1 us
    dot_general x2, matrix products, one_block(): jnp.einsum('qhd,khd->hqk', queries, key_part, preferred_element_type=jnp....  9.53 us
  transfers between devices with their start and end apart: 4, of which 4 were waited for; matrix products, arithmetic and copies ran while one was open for 0% of the time, Pallas kernels for 0%

commit v1 on v0

--- a/solution.py
+++ b/solution.py
@@ -3,6 +3,23 @@
 import jax.numpy as jnp
 from jax import lax
 from jax.sharding import PartitionSpec as P
+
+
+def joined_along(parts, dim):
+    parts = jnp.moveaxis(parts, 0, dim)
+    shape = parts.shape
+    return parts.reshape(*shape[:dim], shape[dim] * shape[dim + 1], *shape[dim + 2 :])
+
+
+def gather_around(array, axis, dim):
+    count = lax.axis_size(axis)
+    upward = [(i, (i + 1) % count) for i in range(count)]
+    blocks = [array]
+    while len(blocks) < count:
+        blocks.append(lax.ppermute(blocks[-1], axis, upward))
+    index = lax.axis_index(axis)
+    blocks = jnp.stack(blocks)[(index - jnp.arange(count)) % count]
+    return joined_along(blocks, dim)
 
 
 def local(tokens, w_qkv, qkv_scale, block_mask, w_out):
@@ -17,7 +34,7 @@
     group_rows = tok_rows * group_count
     block_rows = cycle_count * group_rows // blocks_all
     start_sum = jnp.zeros((group_count, tok_rows, triple, head_cols), jnp.float32)
-    pieces = lax.all_gather(tokens[None], ("ulysses", "tensor"), axis=0, tiled=True)
+    pieces = gather_around(tokens[None], ("ulysses", "tensor"), 0)
 
     def one_shard(which, accum):
         group_id = which // tensor_count

time: 309 us -> 418 us (1.35)
  waiting for transfers between devices: 167 us -> 247 us
  local copies, waits for them, and re-layouts: 27.4 us -> 55.9 us
    ppermute x0 -> x15, waiting for transfers between devices: none -> 173 us  [gather_around(): blocks.append(lax.ppermute(blocks[-1], axis, upward))]
    all_gather x1 -> x0, waiting for transfers between devices: 91.8 us -> none  [local(): lax.all_gather(tokens[None], ('ulysses', 'tensor'), axis=0, tiled=True)]
    unnamed x4 -> x21, local copies, waits for them, and re-layouts: 0.84 us -> 18.5 us
    gather x0 -> x1, local copies, waits for them, and re-layouts: none -> 9.75 us  [gather_around(): blocks = jnp.stack(blocks)[(index - jnp.arange(count)) % count]]
  transfers between devices with their start and end apart: 4 -> 18, of which waited for: 4 -> 18; matrix products, arithmetic and copies ran while one was open for 0% -> 5% of each run, Pallas kernels for 0% -> 0%
where the time goes in v1:
time: 418 us
  waiting for transfers between devices  247 us (59%)
  matrix products  66.6 us (16%)
  local copies, waits for them, and re-layouts  55.9 us (13%)
  blocking collectives  18.7 us (4%)
  other arithmetic  14.2 us (3%)
  between operations  13.2 us (3%)
    ppermute x15, waiting for transfers between devices, gather_around(): blocks.append(lax.ppermute(blocks[-1], axis, upward))  173 us
    dot_general x16, matrix products, one_shard(): jnp.einsum('rd,dcn->rcn', token_part, weights, preferred_element_type=jnp...  41.7 us
    reduce_scatter x1, waiting for transfers between devices, local(): lax.psum_scatter(partial_value.astype(jnp.bfloat16), 'tensor', scatter_di...  32.7 us
    all_gather x1, waiting for transfers between devices, local(): value_all = lax.all_gather(values, 'blk', axis=0, tiled=True)  22.9 us
    all_to_all x1, blocking collectives, local(): lax.all_to_all(grouped, 'ulysses', split_axis=1, concat_axis=0, tiled=True)  18.7 us
    unnamed x21, local copies, waits for them, and re-layouts  18.5 us
    all_gather x1, waiting for transfers between devices, local(): key_all = lax.all_gather(keys, 'blk', axis=0, tiled=True)  17.8 us
    dynamic_slice x16, local copies, waits for them, and re-layouts, one_shard(): current = lax.dynamic_index_in_dim(accum, group_id, 0, keepdims=False)  15.3 us
  transfers between devices with their start and end apart: 18, of which 18 were waited for; matrix products, arithmetic and copies ran while one was open for 5% of the time, Pallas kernels for 0%

profile of v1, /device:TPU:0, one launch (start us, length us, event | category | flops | bytes accessed | tf_op | source)
XLA Modules:
  0.0 417.7 jit_solution(16990001223133629032)
XLA Ops:
  7.0 13.4 %collective-permute-done = bf16[1,256,1280]{2,1,0:T(8,128)(2,1)S(1)} collective-permute-done((bf16[1,256,1280]{2,1,0:T(8,128)(2,1)}, bf16[1,256,1280]{2,1,0:T(8,128)(2,1)S(1)}, u32[]{:S(2)}, u32[]{:S(2)}) %collective-permute-start) | collective-permute-done | bytes 655392 | tf_op jit(solution)/shard_map/ppermute | solution.py:19
  20.5 12.7 %collective-permute-done.1 = bf16[1,256,1280]{2,1,0:T(8,128)(2,1)S(1)} collective-permute-done((bf16[1,256,1280]{2,1,0:T(8,128)(2,1)S(1)}, bf16[1,256,1280]{2,1,0:T(8,128)(2,1)S(1)}, u32[]{:S(2)}, u32[]{:S(2)}) %collective-permute-start.1) | collective-permute-done | bytes 655392 | tf_op jit(solution)/shard_map/ppermute | solution.py:19
  33.2 12.7 %collective-permute-done.2 = bf16[1,256,1280]{2,1,0:T(8,128)(2,1)S(1)} collective-permute-done((bf16[1,256,1280]{2,1,0:T(8,128)(2,1)S(1)}, bf16[1,256,1280]{2,1,0:T(8,128)(2,1)S(1)}, u32[]{:S(2)}, u32[]{:S(2)}) %collective-permute-start.2) | collective-permute-done | bytes 655392 | tf_op jit(solution)/shard_map/ppermute | solution.py:19
  45.9 12.7 %collective-permute-done.3 = bf16[1,256,1280]{2,1,0:T(8,128)(2,1)S(1)} collective-permute-done((bf16[1,256,1280]{2,1,0:T(8,128)(2,1)S(1)}, bf16[1,256,1280]{2,1,0:T(8,128)(2,1)S(1)}, u32[]{:S(2)}, u32[]{:S(2)}) %collective-permute-start.3) | collective-permute-done | bytes 655392 | tf_op jit(solution)/shard_map/ppermute | solution.py:19
  58.6 12.7 %collective-permute-done.4 = bf16[1,256,1280]{2,1,0:T(8,128)(2,1)S(1)} collective-permute-done((bf16[1,256,1280]{2,1,0:T(8,128)(2,1)S(1)}, bf16[1,256,1280]{2,1,0:T(8,128)(2,1)S(1)}, u32[]{:S(2)}, u32[]{:S(2)}) %collective-permute-start.4) | collective-permute-done | bytes 655392 | tf_op jit(solution)/shard_map/ppermute | solution.py:19
  71.3 12.8 %collective-permute-done.5 = bf16[1,256,1280]{2,1,0:T(8,128)(2,1)} collective-permute-done((bf16[1,256,1280]{2,1,0:T(8,128)(2,1)S(1)}, bf16[1,256,1280]{2,1,0:T(8,128)(2,1)}, u32[]{:S(2)}, u32[]{:S(2)}) %collective-permute-start.5) | collective-permute-done | bytes 655392 | tf_op jit(solution)/shard_map/ppermute | solution.py:19
  84.1 12.9 %collective-permute-done.6 = bf16[1,256,1280]{2,1,0:T(8,128)(2,1)S(1)} collective-permute-done((bf16[1,256,1280]{2,1,0:T(8,128)(2,1)}, bf16[1,256,1280]{2,1,0:T(8,128)(2,1)S(1)}, u32[]{:S(2)}, u32[]{:S(2)}) %collective-permute-start.6) | collective-permute-done | bytes 655392 | tf_op jit(solution)/shard_map/ppermute | solution.py:19
  97.8 2.0 bitcast_dynamic-update-slice_fusion.15
  99.8 10.1 %collective-permute-done.7 = bf16[1,256,1280]{2,1,0:T(8,128)(2,1)} collective-permute-done((bf16[1,256,1280]{2,1,0:T(8,128)(2,1)S(1)}, bf16[1,256,1280]{2,1,0:T(8,128)(2,1)}, u32[]{:S(2)}, u32[]{:S(2)}) %collective-permute-start.7) | collective-permute-done | bytes 655392 | tf_op jit(solution)/shard_map/ppermute | solution.py:19
  111.6 11.2 %collective-permute-done.8 = bf16[1,256,1280]{2,1,0:T(8,128)(2,1)S(1)} collective-permute-done((bf16[1,256,1280]{2,1,0:T(8,128)(2,1)}, bf16[1,256,1280]{2,1,0:T(8,128)(2,1)S(1)}, u32[]{:S(2)}, u32[]{:S(2)}) %collective-permute-start.8) | collective-permute-done | bytes 655392 | tf_op jit(solution)/shard_map/ppermute | solution.py:19
  123.7 2.0 bitcast_dynamic-update-slice_fusion.11
  125.7 9.8 %collective-permute-done.9 = bf16[1,256,1280]{2,1,0:T(8,128)(2,1)S(1)} collective-permute-done((bf16[1,256,1280]{2,1,0:T(8,128)(2,1)S(1)}, bf16[1,256,1280]{2,1,0:T(8,128)(2,1)S(1)}, u32[]{:S(2)}, u32[]{:S(2)}) %collective-permute-start.9) | collective-permute-done | bytes 655392 | tf_op jit(solution)/shard_map/ppermute | solution.py:19
  136.3 2.0 bitcast_dynamic-update-slice_fusion.9
  138.3 9.9 %collective-permute-done.10 = bf16[1,256,1280]{2,1,0:T(8,128)(2,1)S(1)} collective-permute-done((bf16[1,256,1280]{2,1,0:T(8,128)(2,1)S(1)}, bf16[1,256,1280]{2,1,0:T(8,128)(2,1)S(1)}, u32[]{:S(2)}, u32[]{:S(2)}) %collective-permute-start.10) | collective-permute-done | bytes 655392 | tf_op jit(solution)/shard_map/ppermute | solution.py:19
  149.1 2.0 bitcast_dynamic-update-slice_fusion.7
  151.1 9.8 %collective-permute-done.11 = bf16[1,256,1280]{2,1,0:T(8,128)(2,1)S(1)} collective-permute-done((bf16[1,256,1280]{2,1,0:T(8,128)(2,1)S(1)}, bf16[1,256,1280]{2,1,0:T(8,128)(2,1)S(1)}, u32[]{:S(2)}, u32[]{:S(2)}) %collective-permute-start.11) | collective-permute-done | bytes 655392 | tf_op jit(solution)/shard_map/ppermute | solution.py:19
  162.7 10.9 %collective-permute-done.12 = bf16[1,256,1280]{2,1,0:T(8,128)(2,1)S(1)} collective-permute-done((bf16[1,256,1280]{2,1,0:T(8,128)(2,1)S(1)}, bf16[1,256,1280]{2,1,0:T(8,128)(2,1)S(1)}, u32[]{:S(2)}, u32[]{:S(2)}) %collective-permute-start.12) | collective-permute-done | bytes 655392 | tf_op jit(solution)/shard_map/ppermute | solution.py:19
  175.4 10.9 %collective-permute-done.13 = bf16[1,256,1280]{2,1,0:T(8,128)(2,1)S(1)} collective-permute-done((bf16[1,256,1280]{2,1,0:T(8,128)(2,1)S(1)}, bf16[1,256,1280]{2,1,0:T(8,128)(2,1)S(1)}, u32[]{:S(2)}, u32[]{:S(2)}) %collective-permute-start.13) | collective-permute-done | bytes 655392 | tf_op jit(solution)/shard_map/ppermute | solution.py:19
  188.1 10.9 %collective-permute-done.14 = bf16[1,256,1280]{2,1,0:T(8,128)(2,1)S(1)} collective-permute-done((bf16[1,256,1280]{2,1,0:T(8,128)(2,1)S(1)}, bf16[1,256,1280]{2,1,0:T(8,128)(2,1)S(1)}, u32[]{:S(2)}, u32[]{:S(2)}) %collective-permute-start.14) | collective-permute-done | bytes 655392 | tf_op jit(solution)/shard_map/ppermute | solution.py:19
  199.9 9.8 %gather_fusion = bf16[16,256,1280]{2,1,0:T(8,128)(2,1)} fusion(bf16[16,256,1280]{2,1,0:T(8,128)(2,1)} %bitcast.25, s32[1024]{0:T(1024)S(1)} %pad_clamp_fusion), kind=kCustom, calls=%fused_computation | custom fusion | bytes 20971584 | tf_op jit(solution)/shard_map/gather | solution.py:21
  209.9 57.5 %while.36 = (s32[]{:T(128)}, f32[4,256,3,256]{3,1,0,2:T(8,128)S(1)}, bf16[16,256,1280]{2,1,0:T(8,128)(2,1)}, bf16[5120,3,256]{2,0,1:T(8,128)(2,1)}, s32[]{:T(128...) while((s32[]{:T(128)}, ...), condition=%wide.region_1.2_spmd, body=%wide.region_0.1_spmd.sunk | while | flops 503513120 | bytes 5768004 | solution.py:48
  209.9 1.0 constant_dynamic-slice_fusion.5
  210.9 2.6 fusion.108
  214.5 2.6 fusion.108
  217.1 1.0 constant_dynamic-slice_fusion.5
  218.1 2.6 fusion.108
  221.7 2.6 fusion.108
  225.3 2.6 fusion.108
  227.9 1.0 constant_dynamic-slice_fusion.5
  228.9 2.6 fusion.108
  232.5 2.6 fusion.108
  235.1 1.0 constant_dynamic-slice_fusion.5
  236.1 2.6 fusion.108
  239.6 2.6 fusion.108
  242.3 1.0 constant_dynamic-slice_fusion.5
  243.2 2.6 fusion.108
  246.8 2.6 fusion.108
  249.5 1.0 constant_dynamic-slice_fusion.5
  250.4 2.6 fusion.108
  254.0 2.6 fusion.108
  257.6 2.6 fusion.108
  261.2 2.6 fusion.108
  264.8 2.6 fusion.108
  267.5 3.1 reshape.270
  270.5 3.0 multiply_convert_fusion
  273.6 2.1 slice_bitcast_fusion
  277.0 17.8 %all-gather.5.cloned.1.call-done = bf16[2048,1,2,128]{3,2,1,0:T(2,128)(2,1)} async-done(((bf16[1024,1,2,128]{3,2,1,0:T(2,128)(2,1)}), bf16[2048,1,2,128]{3,2,1,0:T(2,128)(2,1)}) %all-gather.5.cloned.1.call-update) | async-done | bytes 1048592 | tf_op jit(solution)/shard_map/all_gather | solution.py:76
  294.9 22.9 %all-gather.7.cloned.1.call-done = bf16[2048,1,2,128]{3,2,1,0:T(2,128)(2,1)} async-done(((bf16[1024,1,2,128]{3,2,1,0:T(2,128)(2,1)}), bf16[2048,1,2,128]{3,2,1,0:T(2,128)(2,1)}) %all-gather.7.cloned.1.call-update) | async-done | bytes 1048592 | tf_op jit(solution)/shard_map/all_gather | solution.py:77
  317.7 33.5 %while.37 = (s32[]{:T(128)}, f32[2,1024]{1,0:T(2,128)S(1)}, f32[2,1024]{1,0:T(2,128)S(1)}, f32[2,1024,128]{2,1,0:T(8,128)S(1)}, bf16[2,1024,16]{1,2,0:T(8,128)(2...) while((s32[]{:T(128)}, f32[2,1024]{1,0:T(2,128)S(1)}, ...), condition=%wide.region_5.6_spmd.clone, body=%wide.region_2.5_spmd.clone.sunk | while | flops 1161677824 | bytes 83579104 | solution.py:113
  317.7 1.9 constant_dynamic-slice_fusion.6
  320.3 1.3 fusion.114
  321.6 4.8 %fusion.115 = (f32[2,1024]{1,0:T(2,128)S(1)}, f32[2,1024,1024]{1,2,0:T(8,128)}) fusion(bf16[1024,2,128]{2,0,1:T(8,128)(2,1)S(1)} %get-tuple-element.690, bf16[1024,2,128]{2,1,0:T(2,128)(2,1)S(1)} %get-tuple-element.614, pred[1024,1024]{0,1:T(8,128)(4,1)S(1)} %broadcast_compare_fusion.2, f32[1024,2,1024]{2,0,1:T(8,128)S(1)} %fusion.114), kind=kOutput, calls=%fused_computation.150.clone.1 | convolution fusion | flops 547354624 | bytes 18882560 | tf_op jit(solution)/shard_map/while/body/eval_jaxpr/qhd,khd->hqk/dot_general | solution.py:97
  326.5 4.7 %fusion.117 = f32[2,1024]{1,0:T(2,128)S(1)} fusion(f32[2,1024,1024]{1,2,0:T(8,128)} %get-tuple-element.618, f32[2,1024]{1,0:T(2,128)S(1)} %fusion.116), kind=kLoop, calls=%fused_computation.17.clone.1 | loop fusion | flops 4192256 | bytes 8404992 | tf_op jit(solution)/shard_map/while/body/eval_jaxpr/reduce_sum | solution.py:104
  331.2 1.0 copy-done
  332.2 2.2 fusion.119
  334.5 1.9 constant_dynamic-slice_fusion.6
  337.1 1.3 fusion.114
  338.4 4.8 %fusion.115 = (f32[2,1024]{1,0:T(2,128)S(1)}, f32[2,1024,1024]{1,2,0:T(8,128)}) fusion(bf16[1024,2,128]{2,0,1:T(8,128)(2,1)S(1)} %get-tuple-element.690, bf16[1024,2,128]{2,1,0:T(2,128)(2,1)S(1)} %get-tuple-element.614, pred[1024,1024]{0,1:T(8,128)(4,1)S(1)} %broadcast_compare_fusion.2, f32[1024,2,1024]{2,0,1:T(8,128)S(1)} %fusion.114), kind=kOutput, calls=%fused_computation.150.clone.1 | convolution fusion | flops 547354624 | bytes 18882560 | tf_op jit(solution)/shard_map/while/body/eval_jaxpr/qhd,khd->hqk/dot_general | solution.py:97
  343.2 4.7 %fusion.117 = f32[2,1024]{1,0:T(2,128)S(1)} fusion(f32[2,1024,1024]{1,2,0:T(8,128)} %get-tuple-element.618, f32[2,1024]{1,0:T(2,128)S(1)} %fusion.116), kind=kLoop, calls=%fused_computation.17.clone.1 | loop fusion | flops 4192256 | bytes 8404992 | tf_op jit(solution)/shard_map/while/body/eval_jaxpr/reduce_sum | solution.py:104
  348.0 1.0 copy-done
  349.0 2.2 fusion.119
  351.6 18.7 %all_to_all.15 = bf16[2,4,256,128]{3,2,0,1:T(8,128)(2,1)S(1)} all-to-all(bf16[2,4,256,128]{3,2,0,1:T(8,128)(2,1)S(1)} %copy.27), channel_id=1, replica_groups=mesh['ulysses'=4,'blk'=2,'tensor'=4] {'ulysses'}, dimensions={1} | all-to-all | bytes 1048576 | tf_op jit(solution)/shard_map/all_to_all | solution.py:118
  370.4 8.1 %fusion.68 = bf16[256,5120]{1,0:T(8,128)(2,1)} fusion(bf16[8,256,128]{2,1,0:T(8,128)(2,1)S(1)} %bitcast.109, bf16[8,128,5120]{2,1,0:T(8,128)(2,1)} %bitcast.112), kind=kOutput, calls=%fused_computation.95 | convolution fusion | flops 2685665280 | bytes 13631488 | tf_op jit(solution)/shard_map/grd,gdf->rf/dot_general | solution.py:120
  378.5 32.7 %reduce-scatter.2.cloned.1.call-done = bf16[256,1280]{1,0:T(8,128)(2,1)} async-done(((bf16[256,5120]{1,0:T(8,128)(2,1)}), bf16[256,1280]{1,0:T(8,128)(2,1)}) %reduce-scatter.2.cloned.1.call-update) | async-done | bytes 655376 | tf_op jit(solution)/shard_map/reduce_scatter | solution.py:123
  (74 shorter events, 25.0 us)
Async XLA Ops:
  6.5 288.3 %all-gather.5.cloned.1.call-start = ((), (), s32[]{:S(2)}) async-start(), calls=%async_computation.3 | async-start | bytes 1572864 | tf_op jit(solution)/shard_map/all_gather | solution.py:76
  6.5 13.9 %collective-permute-start = (bf16[1,256,1280]{2,1,0:T(8,128)(2,1)}, bf16[1,256,1280]{2,1,0:T(8,128)(2,1)S(1)}, u32[]{:S(2)}, u32[]{:S(2)}) collective-permute-start(bf16[1,256,1280]{2,1,0:T(8,128)(2,1)} %bitcast.108), channel_id=1, source_target_pairs={{0,1},{1,2},{2,3},{3,8},{8,9},{9,10},{10,11},{11,16},{16,17},{17,1... | collective-permute-start | bytes 1966088 | tf_op jit(solution)/shard_map/ppermute | solution.py:19
  20.5 12.7 %collective-permute-start.1 = (bf16[1,256,1280]{2,1,0:T(8,128)(2,1)S(1)}, bf16[1,256,1280]{2,1,0:T(8,128)(2,1)S(1)}, u32[]{:S(2)}, u32[]{:S(2)}) collective-permute-start(bf16[1,256,1280]{2,1,0:T(8,128)(2,1)S(1)} %collective-permute-done), channel_id=1, source_target_pairs={{0,1},{1,2},{2,3},{3,8},{8,9},{9,10},{10,11},{11,16},{16,17},{17,1... | collective-permute-start | bytes 1966088 | tf_op jit(solution)/shard_map/ppermute | solution.py:19
  33.2 12.7 %collective-permute-start.2 = (bf16[1,256,1280]{2,1,0:T(8,128)(2,1)S(1)}, bf16[1,256,1280]{2,1,0:T(8,128)(2,1)S(1)}, u32[]{:S(2)}, u32[]{:S(2)}) collective-permute-start(bf16[1,256,1280]{2,1,0:T(8,128)(2,1)S(1)} %collective-permute-done.1), channel_id=1, source_target_pairs={{0,1},{1,2},{2,3},{3,8},{8,9},{9,10},{10,11},{11,16},{16,17},{17,1... | collective-permute-start | bytes 1966088 | tf_op jit(solution)/shard_map/ppermute | solution.py:19
  45.9 12.7 %collective-permute-start.3 = (bf16[1,256,1280]{2,1,0:T(8,128)(2,1)S(1)}, bf16[1,256,1280]{2,1,0:T(8,128)(2,1)S(1)}, u32[]{:S(2)}, u32[]{:S(2)}) collective-permute-start(bf16[1,256,1280]{2,1,0:T(8,128)(2,1)S(1)} %collective-permute-done.2), channel_id=1, source_target_pairs={{0,1},{1,2},{2,3},{3,8},{8,9},{9,10},{10,11},{11,16},{16,17},{17,1... | collective-permute-start | bytes 1966088 | tf_op jit(solution)/shard_map/ppermute | solution.py:19
  58.6 12.7 %copy-start.1 = (bf16[1,256,1280]{2,1,0:T(8,128)(2,1)}, bf16[1,256,1280]{2,1,0:T(8,128)(2,1)S(1)}, u32[]{:S(2)}) copy-start(bf16[1,256,1280]{2,1,0:T(8,128)(2,1)S(1)} %collective-permute-done.3) | copy-start | bytes 1966084
  58.6 12.7 %collective-permute-start.4 = (bf16[1,256,1280]{2,1,0:T(8,128)(2,1)S(1)}, bf16[1,256,1280]{2,1,0:T(8,128)(2,1)S(1)}, u32[]{:S(2)}, u32[]{:S(2)}) collective-permute-start(bf16[1,256,1280]{2,1,0:T(8,128)(2,1)S(1)} %collective-permute-done.3), channel_id=1, source_target_pairs={{0,1},{1,2},{2,3},{3,8},{8,9},{9,10},{10,11},{11,16},{16,17},{17,1... | collective-permute-start | bytes 1966088 | tf_op jit(solution)/shard_map/ppermute | solution.py:19
  71.3 12.8 %collective-permute-start.5 = (bf16[1,256,1280]{2,1,0:T(8,128)(2,1)S(1)}, bf16[1,256,1280]{2,1,0:T(8,128)(2,1)}, u32[]{:S(2)}, u32[]{:S(2)}) collective-permute-start(bf16[1,256,1280]{2,1,0:T(8,128)(2,1)S(1)} %collective-permute-done.4), channel_id=1, source_target_pairs={{0,1},{1,2},{2,3},{3,8},{8,9},{9,10},{10,11},{11,16},{16,17},{17,1... | collective-permute-start | bytes 1966088 | tf_op jit(solution)/shard_map/ppermute | solution.py:19
  84.1 12.9 %collective-permute-start.6 = (bf16[1,256,1280]{2,1,0:T(8,128)(2,1)}, bf16[1,256,1280]{2,1,0:T(8,128)(2,1)S(1)}, u32[]{:S(2)}, u32[]{:S(2)}) collective-permute-start(bf16[1,256,1280]{2,1,0:T(8,128)(2,1)} %collective-permute-done.5), channel_id=1, source_target_pairs={{0,1},{1,2},{2,3},{3,8},{8,9},{9,10},{10,11},{11,16},{16,17},{17,1... | collective-permute-start | bytes 1966088 | tf_op jit(solution)/shard_map/ppermute | solution.py:19
  97.0 12.8 %collective-permute-start.7 = (bf16[1,256,1280]{2,1,0:T(8,128)(2,1)S(1)}, bf16[1,256,1280]{2,1,0:T(8,128)(2,1)}, u32[]{:S(2)}, u32[]{:S(2)}) collective-permute-start(bf16[1,256,1280]{2,1,0:T(8,128)(2,1)S(1)} %collective-permute-done.6), channel_id=1, source_target_pairs={{0,1},{1,2},{2,3},{3,8},{8,9},{9,10},{10,11},{11,16},{16,17},{17,1... | collective-permute-start | bytes 1966088 | tf_op jit(solution)/shard_map/ppermute | solution.py:19
  109.8 12.9 %collective-permute-start.8 = (bf16[1,256,1280]{2,1,0:T(8,128)(2,1)}, bf16[1,256,1280]{2,1,0:T(8,128)(2,1)S(1)}, u32[]{:S(2)}, u32[]{:S(2)}) collective-permute-start(bf16[1,256,1280]{2,1,0:T(8,128)(2,1)} %collective-permute-done.7), channel_id=1, source_target_pairs={{0,1},{1,2},{2,3},{3,8},{8,9},{9,10},{10,11},{11,16},{16,17},{17,1... | collective-permute-start | bytes 1966088 | tf_op jit(solution)/shard_map/ppermute | solution.py:19
  122.8 12.7 %collective-permute-start.9 = (bf16[1,256,1280]{2,1,0:T(8,128)(2,1)S(1)}, bf16[1,256,1280]{2,1,0:T(8,128)(2,1)S(1)}, u32[]{:S(2)}, u32[]{:S(2)}) collective-permute-start(bf16[1,256,1280]{2,1,0:T(8,128)(2,1)S(1)} %collective-permute-done.8), channel_id=1, source_target_pairs={{0,1},{1,2},{2,3},{3,8},{8,9},{9,10},{10,11},{11,16},{16,17},{17,1... | collective-permute-start | bytes 1966088 | tf_op jit(solution)/shard_map/ppermute | solution.py:19
  135.5 12.7 %collective-permute-start.10 = (bf16[1,256,1280]{2,1,0:T(8,128)(2,1)S(1)}, bf16[1,256,1280]{2,1,0:T(8,128)(2,1)S(1)}, u32[]{:S(2)}, u32[]{:S(2)}) collective-permute-start(bf16[1,256,1280]{2,1,0:T(8,128)(2,1)S(1)} %collective-permute-done.9), channel_id=1, source_target_pairs={{0,1},{1,2},{2,3},{3,8},{8,9},{9,10},{10,11},{11,16},{16,17},{17,1... | collective-permute-start | bytes 1966088 | tf_op jit(solution)/shard_map/ppermute | solution.py:19
  148.2 12.7 %collective-permute-start.11 = (bf16[1,256,1280]{2,1,0:T(8,128)(2,1)S(1)}, bf16[1,256,1280]{2,1,0:T(8,128)(2,1)S(1)}, u32[]{:S(2)}, u32[]{:S(2)}) collective-permute-start(bf16[1,256,1280]{2,1,0:T(8,128)(2,1)S(1)} %collective-permute-done.10), channel_id=1, source_target_pairs={{0,1},{1,2},{2,3},{3,8},{8,9},{9,10},{10,11},{11,16},{16,17},{17,1... | collective-permute-start | bytes 1966088 | tf_op jit(solution)/shard_map/ppermute | solution.py:19
  160.9 12.7 %collective-permute-start.12 = (bf16[1,256,1280]{2,1,0:T(8,128)(2,1)S(1)}, bf16[1,256,1280]{2,1,0:T(8,128)(2,1)S(1)}, u32[]{:S(2)}, u32[]{:S(2)}) collective-permute-start(bf16[1,256,1280]{2,1,0:T(8,128)(2,1)S(1)} %collective-permute-done.11), channel_id=1, source_target_pairs={{0,1},{1,2},{2,3},{3,8},{8,9},{9,10},{10,11},{11,16},{16,17},{17,1... | collective-permute-start | bytes 1966088 | tf_op jit(solution)/shard_map/ppermute | solution.py:19
  173.6 12.7 %collective-permute-start.13 = (bf16[1,256,1280]{2,1,0:T(8,128)(2,1)S(1)}, bf16[1,256,1280]{2,1,0:T(8,128)(2,1)S(1)}, u32[]{:S(2)}, u32[]{:S(2)}) collective-permute-start(bf16[1,256,1280]{2,1,0:T(8,128)(2,1)S(1)} %collective-permute-done.12), channel_id=1, source_target_pairs={{0,1},{1,2},{2,3},{3,8},{8,9},{9,10},{10,11},{11,16},{16,17},{17,1... | collective-permute-start | bytes 1966088 | tf_op jit(solution)/shard_map/ppermute | solution.py:19
  186.3 12.7 %collective-permute-start.14 = (bf16[1,256,1280]{2,1,0:T(8,128)(2,1)S(1)}, bf16[1,256,1280]{2,1,0:T(8,128)(2,1)S(1)}, u32[]{:S(2)}, u32[]{:S(2)}) collective-permute-start(bf16[1,256,1280]{2,1,0:T(8,128)(2,1)S(1)} %collective-permute-done.13), channel_id=1, source_target_pairs={{0,1},{1,2},{2,3},{3,8},{8,9},{9,10},{10,11},{11,16},{16,17},{17,1... | collective-permute-start | bytes 1966088 | tf_op jit(solution)/shard_map/ppermute | solution.py:19
  267.4 9.2 %copy-start.2 = (s32[2,16,16]{2,1,0:T(8,128)S(1)}, s32[2,16,16]{2,1,0:T(8,128)}, u32[]{:S(2)}) copy-start(s32[2,16,16]{2,1,0:T(8,128)} %param.12) | copy-start | bytes 6148
  275.7 42.0 %all-gather.7.cloned.1.call-start = ((), (), s32[]{:S(2)}) async-start(), calls=%async_computation.4 | async-start | bytes 1572864 | tf_op jit(solution)/shard_map/all_gather | solution.py:77
  276.4 134.7 %reduce-scatter.2.cloned.1.call-start = ((), (), s32[]{:S(2)}) async-start(), calls=%async_computation.2 | async-start | bytes 3276800 | tf_op jit(solution)/shard_map/reduce_scatter | solution.py:123
  326.4 5.8 %copy-start = (f32[2,1024,1024]{1,2,0:T(8,128)S(1)}, f32[2,1024,1024]{1,2,0:T(8,128)}, u32[]{:S(2)}) copy-start(f32[2,1024,1024]{1,2,0:T(8,128)} %get-tuple-element.618) | copy-start | bytes 25165828 | tf_op jit(solution)/shard_map/while
  343.2 5.8 %copy-start = (f32[2,1024,1024]{1,2,0:T(8,128)S(1)}, f32[2,1024,1024]{1,2,0:T(8,128)}, u32[]{:S(2)}) copy-start(f32[2,1024,1024]{1,2,0:T(8,128)} %get-tuple-element.618) | copy-start | bytes 25165828 | tf_op jit(solution)/shard_map/while
Sparse Core Ops, SparseCore 0:
  275.8 19.0 all-gather.4
  296.4 21.2 all-gather.6
  378.6 32.4 reduce-scatter.1
